TPU v7x, 32 devices: a whole 2x2x4 slice. The times are simulated.
32 devices in a mesh: section: 4 (over y, x), fsdp: 8 (over z, core).
Axes of the slice: x: 2, y: 2, z: 4, core: 2. Of those that a mesh axis runs over, the one named last changes fastest.
Arguments:
- enc_states: bfloat16 [8, 4, 1280], P('fsdp'), may hold values from -6 to 6
- clip_frames: int32 [8], replicated, may hold values from 2 to 4, as said below
- clip_offset: int32 [8], replicated, may hold values from 0 to 126, as said below
- ln_gain: float32 [1280], replicated, may hold values from 0.1 to 1.9
- ln_bias: float32 [1280], replicated, may hold values from -0.6 to 0.6
- w_proj: bfloat16 [1280, 8192], P(None, 'fsdp'), may hold values from -0.15625 to 0.15625
- proj_bias: float32 [8192], P('fsdp'), may hold values from -3 to 3
- text_embed: bfloat16 [64, 2, 8192], P(None, None, 'fsdp'), may hold values from -6 to 6
- norm_gain: float32 [4, 8192], P('section'), may hold values from 0.1 to 1.9
- w_gate: bfloat16 [4, 14784, 8192], P('section', 'fsdp'), may hold values from -0.0625 to 0.0625
- w_up: bfloat16 [4, 14784, 8192], P('section', 'fsdp'), may hold values from -0.0625 to 0.0625
- w_down: bfloat16 [4, 14784, 8192], P('section', 'fsdp'), may hold values from -0.046875 to 0.046875
Outputs:
- stream_out: bfloat16 [64, 2, 8192], P('section', None, 'fsdp')
Inputs may be any that keep to these rules, and one draw needn't show every extreme that they name: `clip_frames`: every clip's frame count is even, and some clip has exactly 4 frames. Clip c's live rows occupy stream positions clip_offset[c] to clip_offset[c] + clip_frames[c] / 2 - 1, all inside one microbatch (positions m * 64 to (m + 1) * 64 - 1); no two clips share a position; each microbatch holds 4 clips.
All inputs are finite; a program needn't handle non-finite values.
Results may differ from a plain program's by a relative error of at most 0.015.
Values may be sent and summed in bfloat16 or wider, within the bound.
No kernel may reach another device: no remote copies, remote signals or barrier semaphores. Data moves between devices by JAX's collectives and lax.ppermute only.
A program may use at most 192 MiB of HBM per device.

v0:
```python
import jax
import jax.numpy as jnp
from jax import lax
from jax.sharding import PartitionSpec as P


def from_behind(value, axis, steps):
    count = lax.axis_size(axis)
    initial, last = (max(0, -steps), min(count, count - steps))
    return lax.ppermute(value, axis, [(source, source + steps) for source in range(initial, last)])


def from_root(value, axis, source):
    kept = jnp.where(lax.axis_index(axis) == source, value, 0).astype(value.dtype)
    return lax.psum(kept, axis)


def rms_scaled(stream, gain):
    values = stream.astype(jnp.float32)
    scale = lax.rsqrt(jnp.mean(values * values, axis=-1, keepdims=True) + 1e-06)
    return (values * scale * gain).astype(jnp.bfloat16)


def on_device(
    enc_states,
    clip_frames,
    clip_offset,
    ln_gain,
    ln_bias,
    w_proj,
    proj_bias,
    text_embed,
    norm_gain,
    w_gate,
    w_up,
    w_down,
):
    section_count = lax.axis_size("section")
    section_index = lax.axis_index("section")
    local_clips, frame_len, enc_width = enc_states.shape
    clip_rows = frame_len // 2
    tokens, micro, feat_local = text_embed.shape
    slots = tokens * micro
    pairs = enc_states.astype(jnp.float32).reshape(local_clips, clip_rows, 2, enc_width)
    pooled = 0.5 * (pairs[:, :, 0] + pairs[:, :, 1])
    centre = jnp.mean(pooled, axis=-1, keepdims=True)
    centred = pooled - centre
    spread = jnp.mean(centred * centred, axis=-1, keepdims=True)
    audio_ln = (centred * lax.rsqrt(spread + 1e-05) * ln_gain + ln_bias).astype(jnp.bfloat16)
    audio_ln = audio_ln.reshape(local_clips * clip_rows, enc_width)
    summed = jnp.dot(
        lax.all_gather(audio_ln, "fsdp", axis=0, tiled=True),
        w_proj,
        preferred_element_type=jnp.float32,
    )
    projected = (summed + proj_bias).astype(jnp.bfloat16)
    within = jnp.arange(clip_rows, dtype=jnp.int32)
    live = within[None, :] * 2 < clip_frames[:, None]
    spot = clip_offset[:, None] + within[None, :]
    target = jnp.where(live, spot % tokens * micro + spot // tokens, slots).reshape(-1)
    flags = jnp.zeros((slots,), jnp.int32).at[target].set(1, mode="drop").reshape(tokens, micro)
    placed = jnp.zeros((slots, feat_local), jnp.bfloat16).at[target].set(projected, mode="drop")
    placed = placed.reshape(tokens, micro, feat_local)
    embedded = jnp.where(flags[:, :, None] == 1, placed, text_embed)
    gain = norm_gain[0]
    gate_w = w_gate[0]
    up_w = w_up[0]
    down_w = w_down[0]
    width = gate_w.shape[1]
    dims = (((1,), (1,)), ((), ()))
    group = 1
    waves = micro // group
    turns = waves + section_count - 1
    zero_rows = jnp.zeros((tokens, group, feat_local), jnp.bfloat16)
    incoming = zero_rows
    finished = jnp.zeros((tokens, micro, feat_local), jnp.bfloat16)
    first_section = section_index == 0
    for turn in range(turns):
        if turn < waves:
            fresh = embedded[:, turn * group : (turn + 1) * group]
        else:
            fresh = zero_rows
        current = jnp.where(first_section, fresh, incoming)
        whole = lax.all_gather(current, "fsdp", axis=2, tiled=True)
        layer_normed = rms_scaled(whole, gain).reshape(-1, width)
        gate = lax.dot_general(layer_normed, gate_w, dims, preferred_element_type=jnp.float32)
        up = lax.dot_general(layer_normed, up_w, dims, preferred_element_type=jnp.float32)
        hidden = (jax.nn.silu(gate) * up).astype(jnp.bfloat16)
        partial_sum = jnp.dot(hidden, down_w, preferred_element_type=jnp.float32).reshape(
            tokens, group, width
        )
        branch = lax.psum_scatter(partial_sum, "fsdp", scatter_dimension=2, tiled=True)
        output = (current.astype(jnp.float32) + branch).astype(jnp.bfloat16)
        leaving = turn - (section_count - 1)
        if leaving >= 0:
            finished = finished.at[:, leaving * group : (leaving + 1) * group].set(output)
        if turn + 1 < turns:
            incoming = from_behind(output, "section", 1)
    complete = from_root(finished, "section", section_count - 1)
    rows_each = tokens // section_count
    return lax.dynamic_slice_in_dim(complete, section_index * rows_each, rows_each, 0)


def solution(mesh):
    placed = (
        P("fsdp", None, None),
        P(),
        P(),
        P(),
        P(),
        P(None, "fsdp"),
        P("fsdp"),
        P(None, None, "fsdp"),
        P("section", None),
        P("section", "fsdp", None),
        P("section", "fsdp", None),
        P("section", "fsdp", None),
    )
    return jax.shard_map(
        on_device, mesh=mesh, in_specs=placed, out_specs=P("section", None, "fsdp"), check_vma=False
    )
```

profile of v0, /device:TPU:0, one launch (start us, length us, event | category | flops | bytes accessed | tf_op | source)
XLA Modules:
  0.0 612.4 jit_solution(13028541609225380550)
XLA Ops:
  8.5 15.8 %all-gather = bf16[8,2,1280]{2,1,0:T(2,128)(2,1)S(1)} all-gather(bf16[1,2,1280]{2,1,0:T(2,128)(2,1)S(1)} %fusion.160), channel_id=1, replica_groups=mesh['section'=4,'fsdp'=8] {'fsdp'}, dimensions={0}, use_global_device_ids=true | all-gather | bytes 46080 | tf_op jit(solution)/shard_map/all_gather | solution.py:52
  29.8 23.4 %all-gather.7.cloned.1.call-done = bf16[64,1,8192]{2,0,1:T(8,128)(2,1)} async-done(((bf16[64,1,1024]{2,0,1:T(8,128)(2,1)}), bf16[64,1,8192]{2,0,1:T(8,128)(2,1)}) %all-gather.7.cloned.1.call-update) | async-done | bytes 1048592 | tf_op jit(solution)/shard_map/all_gather | solution.py:84
  53.2 1.6 fusion.85
  54.9 14.8 %fusion.28 = f32[64,1848]{1,0:T(8,128)S(1)} fusion(bf16[1,1848,8192]{2,1,0:T(8,128)(2,1)} %param.25, bf16[64,1,8192]{2,0,1:T(8,128)(2,1)S(1)} %copy-done.2, f32[8192]{0:T(1024)S(1)} %bitcast.133, f32[64]{0:T(128)S(1)} %add_rsqrt_fusion.4), kind=kOutput, calls=%fused_computation.30 | convolution fusion | flops 1939865600 | bytes 31832320 | tf_op jit(solution)/shard_map/dot_general | solution.py:86
  69.7 25.7 %fusion.30 = f32[64,1,8192]{2,0,1:T(8,128)} fusion(bf16[1,1848,8192]{2,1,0:T(8,128)(2,1)} %param.27, bf16[1,1848,8192]{2,1,0:T(8,128)(2,1)} %param.26, f32[64,1848]{1,0:T(8,128)S(1)} %fusion.28, bf16[64,1,8192]{2,0,1:T(8,128)(2,1)S(1)} %copy-done.2, f32[8192]{0:T(1024)S(1)} %bitcast.134, f32[64]{0:T(128)S(1)} %add_rsqrt_fusion.4), kind=kOutput, calls=%fused_computation.32 | convolution fusion | flops 3878343680 | bytes 64207104 | tf_op jit(solution)/shard_map/dot_general | solution.py:89
  95.5 35.7 %reduce-scatter.6.cloned.1.call-done = f32[64,1,1024]{2,0,1:T(8,128)} async-done(((f32[64,1,8192]{2,0,1:T(8,128)}), f32[64,1,1024]{2,0,1:T(8,128)}) %reduce-scatter.6.cloned.1.call-update) | async-done | bytes 262160 | tf_op jit(solution)/shard_map/reduce_scatter | solution.py:92
  132.1 3.4 collective-permute-start
  135.5 2.5 collective-permute-done
  139.1 21.2 %all-gather.9.cloned.1.call-done = bf16[64,1,8192]{2,0,1:T(8,128)(2,1)} async-done(((bf16[64,1,1024]{2,0,1:T(8,128)(2,1)}), bf16[64,1,8192]{2,0,1:T(8,128)(2,1)}) %all-gather.9.cloned.1.call-update) | async-done | bytes 1048592 | tf_op jit(solution)/shard_map/all_gather | solution.py:84
  160.3 1.6 fusion.88
  161.9 14.8 %fusion.26 = f32[64,1848]{1,0:T(8,128)S(1)} fusion(bf16[1,1848,8192]{2,1,0:T(8,128)(2,1)} %param.25, bf16[64,1,8192]{2,0,1:T(8,128)(2,1)S(1)} %copy-done.6, f32[64]{0:T(128)S(1)} %add_rsqrt_fusion.3, f32[8192]{0:T(1024)S(1)} %bitcast.135), kind=kOutput, calls=%fused_computation.28 | convolution fusion | flops 1939865600 | bytes 31832320 | tf_op jit(solution)/shard_map/dot_general | solution.py:86
  176.7 25.7 %fusion.33 = f32[64,1,8192]{2,0,1:T(8,128)} fusion(bf16[1,1848,8192]{2,1,0:T(8,128)(2,1)} %param.27, bf16[1,1848,8192]{2,1,0:T(8,128)(2,1)} %param.26, f32[64,1848]{1,0:T(8,128)S(1)} %fusion.26, bf16[64,1,8192]{2,0,1:T(8,128)(2,1)S(1)} %copy-done.6, f32[64]{0:T(128)S(1)} %add_rsqrt_fusion.3, f32[8192]{0:T(1024)S(1)} %bitcast.136), kind=kOutput, calls=%fused_computation.33 | convolution fusion | flops 3878343680 | bytes 64207104 | tf_op jit(solution)/shard_map/dot_general | solution.py:89
  202.5 35.7 %reduce-scatter.8.cloned.1.call-done = f32[64,1,1024]{2,0,1:T(8,128)} async-done(((f32[64,1,8192]{2,0,1:T(8,128)}), f32[64,1,1024]{2,0,1:T(8,128)}) %reduce-scatter.8.cloned.1.call-update) | async-done | bytes 262160 | tf_op jit(solution)/shard_map/reduce_scatter | solution.py:92
  239.1 3.5 collective-permute-start.1
  242.6 2.5 collective-permute-done.1
  246.4 20.8 %all-gather.11.cloned.1.call-done = bf16[64,1,8192]{2,0,1:T(8,128)(2,1)} async-done(((bf16[64,1,1024]{2,0,1:T(8,128)(2,1)}), bf16[64,1,8192]{2,0,1:T(8,128)(2,1)}) %all-gather.11.cloned.1.call-update) | async-done | bytes 1048592 | tf_op jit(solution)/shard_map/all_gather | solution.py:84
  268.8 14.8 %fusion.24 = f32[64,1848]{1,0:T(8,128)S(1)} fusion(bf16[1,1848,8192]{2,1,0:T(8,128)(2,1)} %param.25, bf16[64,1,8192]{2,0,1:T(8,128)(2,1)S(1)} %copy-done.3, f32[64]{0:T(128)S(1)} %add_rsqrt_fusion.2, f32[8192]{0:T(1024)S(1)} %bitcast.137), kind=kOutput, calls=%fused_computation.26 | convolution fusion | flops 1939865600 | bytes 31832320 | tf_op jit(solution)/shard_map/dot_general | solution.py:86
  283.5 25.7 %fusion.36 = f32[64,1,8192]{2,0,1:T(8,128)} fusion(bf16[1,1848,8192]{2,1,0:T(8,128)(2,1)} %param.27, bf16[1,1848,8192]{2,1,0:T(8,128)(2,1)} %param.26, f32[64,1848]{1,0:T(8,128)S(1)} %fusion.24, bf16[64,1,8192]{2,0,1:T(8,128)(2,1)S(1)} %copy-done.3, f32[64]{0:T(128)S(1)} %add_rsqrt_fusion.2, f32[8192]{0:T(1024)S(1)} %bitcast.138), kind=kOutput, calls=%fused_computation.34 | convolution fusion | flops 3878343680 | bytes 64207104 | tf_op jit(solution)/shard_map/dot_general | solution.py:89
  309.3 35.8 %reduce-scatter.10.cloned.1.call-done = f32[64,1,1024]{2,0,1:T(8,128)} async-done(((f32[64,1,8192]{2,0,1:T(8,128)}), f32[64,1,1024]{2,0,1:T(8,128)}) %reduce-scatter.10.cloned.1.call-update) | async-done | bytes 262160 | tf_op jit(solution)/shard_map/reduce_scatter | solution.py:92
  346.1 3.4 collective-permute-start.2
  349.5 2.5 collective-permute-done.2
  352.9 21.2 %all-gather.13.cloned.1.call-done = bf16[64,1,8192]{2,0,1:T(8,128)(2,1)} async-done(((bf16[64,1,1024]{2,0,1:T(8,128)(2,1)}), bf16[64,1,8192]{2,0,1:T(8,128)(2,1)}) %all-gather.13.cloned.1.call-update) | async-done | bytes 1048592 | tf_op jit(solution)/shard_map/all_gather | solution.py:84
  375.7 14.8 %fusion.22 = f32[64,1848]{1,0:T(8,128)S(1)} fusion(bf16[1,1848,8192]{2,1,0:T(8,128)(2,1)} %param.25, bf16[64,1,8192]{2,0,1:T(8,128)(2,1)S(1)} %copy-done.4, f32[64]{0:T(128)S(1)} %add_rsqrt_fusion.1, f32[8192]{0:T(1024)S(1)} %bitcast.139), kind=kOutput, calls=%fused_computation.24 | convolution fusion | flops 1939865600 | bytes 31832320 | tf_op jit(solution)/shard_map/dot_general | solution.py:86
  390.5 25.7 %fusion.39 = f32[64,1,8192]{2,0,1:T(8,128)} fusion(bf16[1,1848,8192]{2,1,0:T(8,128)(2,1)} %param.27, bf16[1,1848,8192]{2,1,0:T(8,128)(2,1)} %param.26, f32[64,1848]{1,0:T(8,128)S(1)} %fusion.22, bf16[64,1,8192]{2,0,1:T(8,128)(2,1)S(1)} %copy-done.4, f32[64]{0:T(128)S(1)} %add_rsqrt_fusion.1, f32[8192]{0:T(1024)S(1)} %bitcast.140), kind=kOutput, calls=%fused_computation.35 | convolution fusion | flops 3878343680 | bytes 64207104 | tf_op jit(solution)/shard_map/dot_general | solution.py:89
  416.3 35.8 %reduce-scatter.12.cloned.1.call-done = f32[64,1,1024]{2,0,1:T(8,128)} async-done(((f32[64,1,8192]{2,0,1:T(8,128)}), f32[64,1,1024]{2,0,1:T(8,128)}) %reduce-scatter.12.cloned.1.call-update) | async-done | bytes 262160 | tf_op jit(solution)/shard_map/reduce_scatter | solution.py:92
  453.1 3.3 collective-permute-start.3
  456.3 2.5 collective-permute-done.3
  459.8 21.2 %all-gather.15.cloned.1.call-done = bf16[64,1,8192]{2,0,1:T(8,128)(2,1)} async-done(((bf16[64,1,1024]{2,0,1:T(8,128)(2,1)}), bf16[64,1,8192]{2,0,1:T(8,128)(2,1)}) %all-gather.15.cloned.1.call-update) | async-done | bytes 1048592 | tf_op jit(solution)/shard_map/all_gather | solution.py:84
  482.6 14.8 %fusion.20 = f32[64,1848]{1,0:T(8,128)S(1)} fusion(bf16[1,1848,8192]{2,1,0:T(8,128)(2,1)} %param.25, bf16[64,1,8192]{2,0,1:T(8,128)(2,1)S(1)} %copy-done.5, f32[64]{0:T(128)S(1)} %add_rsqrt_fusion, f32[8192]{0:T(1024)S(1)} %bitcast.141), kind=kOutput, calls=%fused_computation.22 | convolution fusion | flops 1939865600 | bytes 31832320 | tf_op jit(solution)/shard_map/dot_general | solution.py:86
  497.4 26.2 %fusion.42 = f32[64,1,8192]{2,0,1:T(8,128)} fusion(bf16[1,1848,8192]{2,1,0:T(8,128)(2,1)} %param.27, bf16[1,1848,8192]{2,1,0:T(8,128)(2,1)} %param.26, f32[64,1848]{1,0:T(8,128)S(1)} %fusion.20, bf16[64,1,8192]{2,0,1:T(8,128)(2,1)} %all-gather.15.cloned.1.call-done, f32[64]{0:T(128)S(1)} %add_rsqrt_fusion, f32[8192]{0:T(1024)S(1)} %bitcast.142), kind=kOutput, calls=%fused_computation.36 | convolution fusion | flops 3878343680 | bytes 64207104 | tf_op jit(solution)/shard_map/dot_general | solution.py:89
  523.7 35.8 %reduce-scatter.14.cloned.1.call-done = f32[64,1,1024]{2,0,1:T(8,128)} async-done(((f32[64,1,8192]{2,0,1:T(8,128)}), f32[64,1,1024]{2,0,1:T(8,128)}) %reduce-scatter.14.cloned.1.call-update) | async-done | bytes 262160 | tf_op jit(solution)/shard_map/reduce_scatter | solution.py:92
  561.2 42.9 %all-reduce.2.cloned.1.call-done = bf16[64,2,1024]{2,0,1:T(8,128)(2,1)} async-done(((bf16[64,2,1024]{2,0,1:T(8,128)(2,1)}), bf16[64,2,1024]{2,0,1:T(8,128)(2,1)}) %all-reduce.2.cloned.1.call-update) | async-done | bytes 262160 | tf_op jit(solution)/shard_map/psum | solution.py:15
  (85 shorter events, 23.9 us)
Async XLA Ops:
  6.5 19.4 %copy-start = (bf16[1280,1024]{1,0:T(8,128)(2,1)S(1)}, bf16[1280,1024]{1,0:T(8,128)(2,1)}, u32[]{:S(2)}) copy-start(bf16[1280,1024]{1,0:T(8,128)(2,1)} %param.21) | copy-start | bytes 7864324
  6.5 22.4 %copy-start.9 = (bf16[64,2,1024]{2,1,0:T(2,128)(2,1)S(1)}, bf16[64,2,1024]{2,1,0:T(2,128)(2,1)}, u32[]{:S(2)}) copy-start(bf16[64,2,1024]{2,1,0:T(2,128)(2,1)} %param.23) | copy-start | bytes 786436
  6.5 46.7 %all-gather.7.cloned.1.call-start = ((), (), s32[]{:S(2)}) async-start(), calls=%async_computation.5 | async-start | bytes 1179648 | tf_op jit(solution)/shard_map/all_gather | solution.py:84
  27.1 27.7 %copy-start.7 = (f32[1,8192]{1,0:T(1,128)S(1)}, f32[1,8192]{1,0:T(1,128)}, u32[]{:S(2)}) copy-start(f32[1,8192]{1,0:T(1,128)} %param.24) | copy-start | bytes 98308
  29.8 101.3 %reduce-scatter.6.cloned.1.call-start = ((), (), s32[]{:S(2)}) async-start(), calls=%async_computation.6 | async-start | bytes 2359296 | tf_op jit(solution)/shard_map/reduce_scatter | solution.py:92
  53.2 1.6 copy-start.2
  95.4 64.8 %all-gather.9.cloned.1.call-start = ((), (), s32[]{:S(2)}) async-start(), calls=%async_computation.7 | async-start | bytes 1179648 | tf_op jit(solution)/shard_map/all_gather | solution.py:84
  132.1 5.9 collective-permute-start
  138.7 99.4 %reduce-scatter.8.cloned.1.call-start = ((), (), s32[]{:S(2)}) async-start(), calls=%async_computation.8 | async-start | bytes 2359296 | tf_op jit(solution)/shard_map/reduce_scatter | solution.py:92
  160.3 1.6 copy-start.6
  202.4 35.8 %copy-start.8 = (bf16[64,1,1024]{2,0,1:T(8,128)(2,1)S(1)}, bf16[64,1,1024]{2,0,1:T(8,128)(2,1)}, u32[]{:S(2)}) copy-start(bf16[64,1,1024]{2,0,1:T(8,128)(2,1)} %slice_select_fusion.1) | copy-start | bytes 393220
  202.4 64.7 %all-gather.11.cloned.1.call-start = ((), (), s32[]{:S(2)}) async-start(), calls=%async_computation.9 | async-start | bytes 1179648 | tf_op jit(solution)/shard_map/all_gather | solution.py:84
  239.1 6.0 collective-permute-start.1
  245.8 99.4 %reduce-scatter.10.cloned.1.call-start = ((), (), s32[]{:S(2)}) async-start(), calls=%async_computation.10 | async-start | bytes 2359296 | tf_op jit(solution)/shard_map/reduce_scatter | solution.py:92
  267.1 1.6 copy-start.3
  309.3 64.8 %all-gather.13.cloned.1.call-start = ((), (), s32[]{:S(2)}) async-start(), calls=%async_computation.11 | async-start | bytes 1179648 | tf_op jit(solution)/shard_map/all_gather | solution.py:84
  346.1 5.9 collective-permute-start.2
  352.7 99.4 %reduce-scatter.12.cloned.1.call-start = ((), (), s32[]{:S(2)}) async-start(), calls=%async_computation.12 | async-start | bytes 2359296 | tf_op jit(solution)/shard_map/reduce_scatter | solution.py:92
  374.1 1.6 copy-start.4
  416.2 64.8 %all-gather.15.cloned.1.call-start = ((), (), s32[]{:S(2)}) async-start(), calls=%async_computation.13 | async-start | bytes 1179648 | tf_op jit(solution)/shard_map/all_gather | solution.py:84
  453.1 5.8 collective-permute-start.3
  459.5 100.0 %reduce-scatter.14.cloned.1.call-start = ((), (), s32[]{:S(2)}) async-start(), calls=%async_computation.14 | async-start | bytes 2359296 | tf_op jit(solution)/shard_map/reduce_scatter | solution.py:92
  481.0 1.6 copy-start.5
  497.4 108.2 %copy-start.1 = (bf16[1280,1024]{1,0:T(8,128)(2,1)S(1)}, bf16[1280,1024]{1,0:T(8,128)(2,1)}, u32[]{:S(2)}) copy-start(bf16[1280,1024]{1,0:T(8,128)(2,1)} %param.21) | copy-start | bytes 7864324
  523.6 80.5 %all-reduce.2.cloned.1.call-start = ((), (), s32[]{:S(2)}) async-start(), calls=%async_computation.15 | async-start | bytes 524288 | tf_op jit(solution)/shard_map/psum | solution.py:15
Sparse Core Ops, SparseCore 0:
  29.9 23.2 all-gather.6
  95.5 35.5 reduce-scatter.5
  138.8 21.3 all-gather.8
  202.5 35.5 reduce-scatter.7
  245.9 21.1 all-gather.10
  309.4 35.6 reduce-scatter.9
  352.8 21.2 all-gather.12
  416.3 35.6 reduce-scatter.11
  459.6 21.2 all-gather.14
  523.7 35.6 reduce-scatter.13
  562.4 41.6 all-reduce.1
where the time goes:
time: 620 us; the launch traced here: 612 us
  waiting for transfers between devices  340 us (55%)
  matrix products  204 us (33%)
  other arithmetic  19.8 us (3%)
  blocking collectives  15.8 us (3%)
  starting transfers between devices  15.1 us (2%)
  between operations  13.8 us (2%)
    reduce_scatter x5, waiting for transfers between devices, on_device(): lax.psum_scatter(partial_sum, 'fsdp', scatter_dimension=2, tiled=True)  179 us
    dot_general x5, matrix products, on_device(): jnp.dot(hidden, down_w, preferred_element_type=jnp.float32)  129 us
    all_gather x5, waiting for transfers between devices, on_device(): whole = lax.all_gather(current, 'fsdp', axis=2, tiled=True)  108 us
    dot_general x5, matrix products, on_device(): lax.dot_general(layer_normed, gate_w, dims, preferred_element_type=jnp.fl...  73.8 us
    psum x1, waiting for transfers between devices, from_root(): return lax.psum(kept, axis)  42.9 us
    all_gather x1, blocking collectives, on_device(): lax.all_gather(audio_ln, 'fsdp', axis=0, tiled=True)  15.8 us
    ppermute x4, starting transfers between devices, from_behind(): lax.ppermute(value, axis, [(source, source + steps) for source in range(i...  13.5 us
  transfers between devices with their start and end apart: 15, of which 15 were waited for; matrix products, arithmetic and copies ran while one was open for 0% of the time, Pallas kernels for 0%

commit v1 on v0

--- a/solution.py
+++ b/solution.py
@@ -81,7 +81,7 @@
         else:
             fresh = zero_rows
         current = jnp.where(first_section, fresh, incoming)
-        whole = lax.all_gather(current, "fsdp", axis=2, tiled=True)
+        whole = jnp.concatenate(lax.all_gather(current, "fsdp"), axis=2)
         layer_normed = rms_scaled(whole, gain).reshape(-1, width)
         gate = lax.dot_general(layer_normed, gate_w, dims, preferred_element_type=jnp.float32)
         up = lax.dot_general(layer_normed, up_w, dims, preferred_element_type=jnp.float32)

time: 620 us -> 647 us (1.044)
  local copies, waits for them, and re-layouts: 4.38 us -> 27.1 us
  other arithmetic: 19.8 us -> 26.9 us
    convert_element_type x0 -> x10, local copies, waits for them, and re-layouts: none -> 21.6 us  [rms_scaled(): values = stream.astype(jnp.float32)]
    convert_element_type x0 -> x5, other arithmetic: none -> 7.34 us  [rms_scaled(): values = stream.astype(jnp.float32)]
where the time goes in v1:
time: 647 us; the launch traced here: 640 us
  waiting for transfers between devices  340 us (53%)
  matrix products  201 us (31%)
  local copies, waits for them, and re-layouts  27.1 us (4%)
  other arithmetic  26.9 us (4%)
  blocking collectives  15.8 us (2%)
  starting transfers between devices  14.9 us (2%)
  between operations  13.8 us (2%)
    reduce_scatter x5, waiting for transfers between devices, on_device(): lax.psum_scatter(partial_sum, 'fsdp', scatter_dimension=2, tiled=True)  179 us
    dot_general x5, matrix products, on_device(): jnp.dot(hidden, down_w, preferred_element_type=jnp.float32)  129 us
    all_gather x5, waiting for transfers between devices, on_device(): whole = jnp.concatenate(lax.all_gather(current, 'fsdp'), axis=2)  108 us
    dot_general x5, matrix products, on_device(): lax.dot_general(layer_normed, gate_w, dims, preferred_element_type=jnp.fl...  71 us
    psum x1, waiting for transfers between devices, from_root(): return lax.psum(kept, axis)  42.9 us
    convert_element_type x10, local copies, waits for them, and re-layouts, rms_scaled(): values = stream.astype(jnp.float32)  21.6 us
    all_gather x1, blocking collectives, on_device(): lax.all_gather(audio_ln, 'fsdp', axis=0, tiled=True)  15.8 us
    ppermute x4, starting transfers between devices, from_behind(): lax.ppermute(value, axis, [(source, source + steps) for source in range(i...  13.3 us
  transfers between devices with their start and end apart: 15, of which 15 were waited for; matrix products, arithmetic and copies ran while one was open for 0% of the time, Pallas kernels for 0%

profile of v1, /device:TPU:0, one launch (start us, length us, event | category | flops | bytes accessed | tf_op | source)
XLA Modules:
  0.0 639.7 jit_solution(10589703348239563159)
XLA Ops:
  11.1 15.8 %all-gather.5 = bf16[8,2,1280]{2,1,0:T(2,128)(2,1)S(1)} all-gather(bf16[1,2,1280]{2,1,0:T(2,128)(2,1)S(1)} %fusion.130), channel_id=1, replica_groups=mesh['section'=4,'fsdp'=8] {'fsdp'}, dimensions={0}, use_global_device_ids=true | all-gather | bytes 46080 | tf_op jit(solution)/shard_map/all_gather | solution.py:52
  29.9 23.4 %all-gather.12.cloned.1.call-done = bf16[512,1,1024]{2,0,1:T(8,128)(2,1)} async-done(((bf16[64,1,1024]{2,0,1:T(8,128)(2,1)}), bf16[512,1,1024]{2,0,1:T(8,128)(2,1)}) %all-gather.12.cloned.1.call-update) | async-done | bytes 1048592 | tf_op jit(solution)/shard_map/all_gather | solution.py:84
  56.3 2.6 copy.60
  60.6 14.2 %fusion.28 = f32[64,1848]{1,0:T(8,128)S(1)} fusion(bf16[1,1848,8192]{2,1,0:T(8,128)(2,1)} %param.25, f32[64,1,1,1,1,1,8192]{6,0,5,4,3,2,1:T(8,128)S(1)} %reshape.901, f32[8192]{0:T(1024)S(1)} %bitcast.185, f32[64]{0:T(128)S(1)} %add_rsqrt_fusion.4), kind=kOutput, calls=%fused_computation.30 | convolution fusion | flops 1939341312 | bytes 32880896 | tf_op jit(solution)/shard_map/dot_general | solution.py:86
  74.8 25.7 %fusion.30 = f32[64,1,8192]{2,0,1:T(8,128)} fusion(bf16[1,1848,8192]{2,1,0:T(8,128)(2,1)} %param.27, bf16[1,1848,8192]{2,1,0:T(8,128)(2,1)} %param.26, f32[64,1848]{1,0:T(8,128)S(1)} %fusion.28, f32[64,1,1,1,1,1,8192]{6,0,5,4,3,2,1:T(8,128)S(1)} %reshape.901, f32[8192]{0:T(1024)S(1)} %bitcast.186, f32[64]{0:T(128)S(1)} %add_rsqrt_fusion.4), kind=kOutput, calls=%fused_computation.32 | convolution fusion | flops 3877819392 | bytes 65255680 | tf_op jit(solution)/shard_map/dot_general | solution.py:89
  100.6 35.8 %reduce-scatter.6.cloned.1.call-done = f32[64,1,1024]{2,0,1:T(8,128)} async-done(((f32[64,1,8192]{2,0,1:T(8,128)}), f32[64,1,1024]{2,0,1:T(8,128)}) %reduce-scatter.6.cloned.1.call-update) | async-done | bytes 262160 | tf_op jit(solution)/shard_map/reduce_scatter | solution.py:92
  137.3 3.3 collective-permute-start
  144.2 21.1 %all-gather.14.cloned.1.call-done = bf16[512,1,1024]{2,0,1:T(8,128)(2,1)} async-done(((bf16[64,1,1024]{2,0,1:T(8,128)(2,1)}), bf16[512,1,1024]{2,0,1:T(8,128)(2,1)}) %all-gather.14.cloned.1.call-update) | async-done | bytes 1048592 | tf_op jit(solution)/shard_map/all_gather | solution.py:84
  168.3 2.6 copy.59
  172.7 14.2 %fusion.26 = f32[64,1848]{1,0:T(8,128)S(1)} fusion(bf16[1,1848,8192]{2,1,0:T(8,128)(2,1)} %param.25, f32[64,1,1,1,1,1,8192]{6,0,5,4,3,2,1:T(8,128)S(1)} %reshape.902, f32[64]{0:T(128)S(1)} %add_rsqrt_fusion.3, f32[8192]{0:T(1024)S(1)} %bitcast.187), kind=kOutput, calls=%fused_computation.28 | convolution fusion | flops 1939341312 | bytes 32880896 | tf_op jit(solution)/shard_map/dot_general | solution.py:86
  186.9 25.7 %fusion.33 = f32[64,1,8192]{2,0,1:T(8,128)} fusion(bf16[1,1848,8192]{2,1,0:T(8,128)(2,1)} %param.27, bf16[1,1848,8192]{2,1,0:T(8,128)(2,1)} %param.26, f32[64,1848]{1,0:T(8,128)S(1)} %fusion.26, f32[64,1,1,1,1,1,8192]{6,0,5,4,3,2,1:T(8,128)S(1)} %reshape.902, f32[64]{0:T(128)S(1)} %add_rsqrt_fusion.3, f32[8192]{0:T(1024)S(1)} %bitcast.188), kind=kOutput, calls=%fused_computation.33 | convolution fusion | flops 3877819392 | bytes 65255680 | tf_op jit(solution)/shard_map/dot_general | solution.py:89
  212.6 35.7 %reduce-scatter.8.cloned.1.call-done = f32[64,1,1024]{2,0,1:T(8,128)} async-done(((f32[64,1,8192]{2,0,1:T(8,128)}), f32[64,1,1024]{2,0,1:T(8,128)}) %reduce-scatter.8.cloned.1.call-update) | async-done | bytes 262160 | tf_op jit(solution)/shard_map/reduce_scatter | solution.py:92
  249.4 3.4 collective-permute-start.1
  252.7 2.5 collective-permute-done.1
  256.5 20.9 %all-gather.16.cloned.1.call-done = bf16[512,1,1024]{2,0,1:T(8,128)(2,1)} async-done(((bf16[64,1,1024]{2,0,1:T(8,128)(2,1)}), bf16[512,1,1024]{2,0,1:T(8,128)(2,1)}) %all-gather.16.cloned.1.call-update) | async-done | bytes 1048592 | tf_op jit(solution)/shard_map/all_gather | solution.py:84
  280.4 2.6 copy.58
  284.7 14.2 %fusion.24 = f32[64,1848]{1,0:T(8,128)S(1)} fusion(bf16[1,1848,8192]{2,1,0:T(8,128)(2,1)} %param.25, f32[64,1,1,1,1,1,8192]{6,0,5,4,3,2,1:T(8,128)S(1)} %reshape.903, f32[64]{0:T(128)S(1)} %add_rsqrt_fusion.2, f32[8192]{0:T(1024)S(1)} %bitcast.189), kind=kOutput, calls=%fused_computation.26 | convolution fusion | flops 1939341312 | bytes 32880896 | tf_op jit(solution)/shard_map/dot_general | solution.py:86
  299.0 25.7 %fusion.36 = f32[64,1,8192]{2,0,1:T(8,128)} fusion(bf16[1,1848,8192]{2,1,0:T(8,128)(2,1)} %param.27, bf16[1,1848,8192]{2,1,0:T(8,128)(2,1)} %param.26, f32[64,1848]{1,0:T(8,128)S(1)} %fusion.24, f32[64,1,1,1,1,1,8192]{6,0,5,4,3,2,1:T(8,128)S(1)} %reshape.903, f32[64]{0:T(128)S(1)} %add_rsqrt_fusion.2, f32[8192]{0:T(1024)S(1)} %bitcast.190), kind=kOutput, calls=%fused_computation.34 | convolution fusion | flops 3877819392 | bytes 65255680 | tf_op jit(solution)/shard_map/dot_general | solution.py:89
  324.7 35.8 %reduce-scatter.10.cloned.1.call-done = f32[64,1,1024]{2,0,1:T(8,128)} async-done(((f32[64,1,8192]{2,0,1:T(8,128)}), f32[64,1,1024]{2,0,1:T(8,128)}) %reduce-scatter.10.cloned.1.call-update) | async-done | bytes 262160 | tf_op jit(solution)/shard_map/reduce_scatter | solution.py:92
  361.5 3.3 collective-permute-start.2
  368.2 21.4 %all-gather.18.cloned.1.call-done = bf16[512,1,1024]{2,0,1:T(8,128)(2,1)} async-done(((bf16[64,1,1024]{2,0,1:T(8,128)(2,1)}), bf16[512,1,1024]{2,0,1:T(8,128)(2,1)}) %all-gather.18.cloned.1.call-update) | async-done | bytes 1048592 | tf_op jit(solution)/shard_map/all_gather | solution.py:84
  392.6 2.6 copy.57
  396.9 14.2 %fusion.22 = f32[64,1848]{1,0:T(8,128)S(1)} fusion(bf16[1,1848,8192]{2,1,0:T(8,128)(2,1)} %param.25, f32[64,1,1,1,1,1,8192]{6,0,5,4,3,2,1:T(8,128)S(1)} %reshape.904, f32[64]{0:T(128)S(1)} %add_rsqrt_fusion.1, f32[8192]{0:T(1024)S(1)} %bitcast.191), kind=kOutput, calls=%fused_computation.24 | convolution fusion | flops 1939341312 | bytes 32880896 | tf_op jit(solution)/shard_map/dot_general | solution.py:86
  411.1 25.7 %fusion.39 = f32[64,1,8192]{2,0,1:T(8,128)} fusion(bf16[1,1848,8192]{2,1,0:T(8,128)(2,1)} %param.27, bf16[1,1848,8192]{2,1,0:T(8,128)(2,1)} %param.26, f32[64,1848]{1,0:T(8,128)S(1)} %fusion.22, f32[64,1,1,1,1,1,8192]{6,0,5,4,3,2,1:T(8,128)S(1)} %reshape.904, f32[64]{0:T(128)S(1)} %add_rsqrt_fusion.1, f32[8192]{0:T(1024)S(1)} %bitcast.192), kind=kOutput, calls=%fused_computation.35 | convolution fusion | flops 3877819392 | bytes 65255680 | tf_op jit(solution)/shard_map/dot_general | solution.py:89
  436.9 35.8 %reduce-scatter.12.cloned.1.call-done = f32[64,1,1024]{2,0,1:T(8,128)} async-done(((f32[64,1,8192]{2,0,1:T(8,128)}), f32[64,1,1024]{2,0,1:T(8,128)}) %reduce-scatter.12.cloned.1.call-update) | async-done | bytes 262160 | tf_op jit(solution)/shard_map/reduce_scatter | solution.py:92
  473.6 3.4 collective-permute-start.3
  480.5 21.1 %all-gather.20.cloned.1.call-done = bf16[512,1,1024]{2,0,1:T(8,128)(2,1)} async-done(((bf16[64,1,1024]{2,0,1:T(8,128)(2,1)}), bf16[512,1,1024]{2,0,1:T(8,128)(2,1)}) %all-gather.20.cloned.1.call-update) | async-done | bytes 1048592 | tf_op jit(solution)/shard_map/all_gather | solution.py:84
  504.6 2.6 copy.56
  510.2 14.2 %fusion.20 = f32[64,1848]{1,0:T(8,128)S(1)} fusion(bf16[1,1848,8192]{2,1,0:T(8,128)(2,1)} %param.25, f32[64,1,1,1,1,1,8192]{6,0,5,4,3,2,1:T(8,128)S(1)} %reshape.905, f32[64]{0:T(128)S(1)} %add_rsqrt_fusion, f32[8192]{0:T(1024)S(1)} %bitcast.193), kind=kOutput, calls=%fused_computation.22 | convolution fusion | flops 1939341312 | bytes 32880896 | tf_op jit(solution)/shard_map/dot_general | solution.py:86
  524.5 26.5 %fusion.42 = f32[64,1,8192]{2,0,1:T(8,128)} fusion(bf16[1,1848,8192]{2,1,0:T(8,128)(2,1)} %param.27, bf16[1,1848,8192]{2,1,0:T(8,128)(2,1)} %param.26, f32[64,1848]{1,0:T(8,128)S(1)} %fusion.20, f32[64,1,1,1,1,1,8192]{6,0,5,4,3,2,1:T(8,128)} %copy-done.2, f32[64]{0:T(128)S(1)} %add_rsqrt_fusion, f32[8192]{0:T(1024)S(1)} %bitcast.194), kind=kOutput, calls=%fused_computation.36 | convolution fusion | flops 3877819392 | bytes 65255680 | tf_op jit(solution)/shard_map/dot_general | solution.py:89
  551.1 35.7 %reduce-scatter.14.cloned.1.call-done = f32[64,1,1024]{2,0,1:T(8,128)} async-done(((f32[64,1,8192]{2,0,1:T(8,128)}), f32[64,1,1024]{2,0,1:T(8,128)}) %reduce-scatter.14.cloned.1.call-update) | async-done | bytes 262160 | tf_op jit(solution)/shard_map/reduce_scatter | solution.py:92
  588.5 42.9 %all-reduce.2.cloned.1.call-done = bf16[64,2,1024]{2,0,1:T(8,128)(2,1)} async-done(((bf16[64,2,1024]{2,0,1:T(8,128)(2,1)}), bf16[64,2,1024]{2,0,1:T(8,128)(2,1)}) %all-reduce.2.cloned.1.call-update) | async-done | bytes 262160 | tf_op jit(solution)/shard_map/psum | solution.py:15
  (92 shorter events, 51.6 us)
Async XLA Ops:
  6.5 20.4 %copy-start = (bf16[1280,1024]{1,0:T(8,128)(2,1)S(1)}, bf16[1280,1024]{1,0:T(8,128)(2,1)}, u32[]{:S(2)}) copy-start(bf16[1280,1024]{1,0:T(8,128)(2,1)} %param.21) | copy-start | bytes 7864324
  6.5 22.4 %copy-start.5 = (bf16[64,2,1024]{2,1,0:T(2,128)(2,1)S(1)}, bf16[64,2,1024]{2,1,0:T(2,128)(2,1)}, u32[]{:S(2)}) copy-start(bf16[64,2,1024]{2,1,0:T(2,128)(2,1)} %param.23) | copy-start | bytes 786436
  6.5 46.7 %all-gather.12.cloned.1.call-start = ((), (), s32[]{:S(2)}) async-start(), calls=%async_computation.11 | async-start | bytes 1179648 | tf_op jit(solution)/shard_map/all_gather | solution.py:84
  29.8 106.5 %reduce-scatter.6.cloned.1.call-start = ((), (), s32[]{:S(2)}) async-start(), calls=%async_computation.5 | async-start | bytes 2359296 | tf_op jit(solution)/shard_map/reduce_scatter | solution.py:92
  58.8 1.8 copy-start.3
  100.5 64.8 %all-gather.14.cloned.1.call-start = ((), (), s32[]{:S(2)}) async-start(), calls=%async_computation.12 | async-start | bytes 1179648 | tf_op jit(solution)/shard_map/all_gather | solution.py:84
  137.3 5.8 collective-permute-start
  143.8 104.5 %reduce-scatter.8.cloned.1.call-start = ((), (), s32[]{:S(2)}) async-start(), calls=%async_computation.6 | async-start | bytes 2359296 | tf_op jit(solution)/shard_map/reduce_scatter | solution.py:92
  212.6 35.8 %copy-start.4 = (bf16[64,1,1024]{2,0,1:T(8,128)(2,1)S(1)}, bf16[64,1,1024]{2,0,1:T(8,128)(2,1)}, u32[]{:S(2)}) copy-start(bf16[64,1,1024]{2,0,1:T(8,128)(2,1)} %slice_select_fusion.1) | copy-start | bytes 393220
  212.6 64.8 %all-gather.16.cloned.1.call-start = ((), (), s32[]{:S(2)}) async-start(), calls=%async_computation.13 | async-start | bytes 1179648 | tf_op jit(solution)/shard_map/all_gather | solution.py:84
  249.4 5.9 collective-permute-start.1
  255.9 104.6 %reduce-scatter.10.cloned.1.call-start = ((), (), s32[]{:S(2)}) async-start(), calls=%async_computation.7 | async-start | bytes 2359296 | tf_op jit(solution)/shard_map/reduce_scatter | solution.py:92
  324.7 64.9 %all-gather.18.cloned.1.call-start = ((), (), s32[]{:S(2)}) async-start(), calls=%async_computation.14 | async-start | bytes 1179648 | tf_op jit(solution)/shard_map/all_gather | solution.py:84
  361.5 5.8 collective-permute-start.2
  368.0 104.7 %reduce-scatter.12.cloned.1.call-start = ((), (), s32[]{:S(2)}) async-start(), calls=%async_computation.8 | async-start | bytes 2359296 | tf_op jit(solution)/shard_map/reduce_scatter | solution.py:92
  436.8 64.8 %all-gather.20.cloned.1.call-start = ((), (), s32[]{:S(2)}) async-start(), calls=%async_computation.15 | async-start | bytes 1179648 | tf_op jit(solution)/shard_map/all_gather | solution.py:84
  473.6 5.9 collective-permute-start.3
  480.2 106.5 %reduce-scatter.14.cloned.1.call-start = ((), (), s32[]{:S(2)}) async-start(), calls=%async_computation.9 | async-start | bytes 2359296 | tf_op jit(solution)/shard_map/reduce_scatter | solution.py:92
  508.9 1.3 copy-start.2
  524.4 108.5 %copy-start.1 = (bf16[1280,1024]{1,0:T(8,128)(2,1)S(1)}, bf16[1280,1024]{1,0:T(8,128)(2,1)}, u32[]{:S(2)}) copy-start(bf16[1280,1024]{1,0:T(8,128)(2,1)} %param.21) | copy-start | bytes 7864324
  551.0 80.4 %all-reduce.2.cloned.1.call-start = ((), (), s32[]{:S(2)}) async-start(), calls=%async_computation.10 | async-start | bytes 524288 | tf_op jit(solution)/shard_map/psum | solution.py:15
Sparse Core Ops, SparseCore 0:
  29.9 23.2 all-gather.11
  100.7 35.6 reduce-scatter.5
  144.0 21.3 all-gather.13
  212.7 35.6 reduce-scatter.7
  256.0 21.3 all-gather.15
  324.8 35.6 reduce-scatter.9
  368.1 21.4 all-gather.17
  437.0 35.6 reduce-scatter.11
  480.3 21.2 all-gather.19
  551.1 35.5 reduce-scatter.13
  589.7 41.6 all-reduce.1
